TPU v7x, 256 devices: a whole 4x4x8 slice. The times are simulated.
256 devices in a mesh: row: 32 (over y, x, core), col: 8 (over z).
Axes of the slice: x: 4, y: 4, z: 8, core: 2. Of those that a mesh axis runs over, the one named last changes fastest.
Arguments:
- inputs: bfloat16 [4096, 5120], P('row', 'col'), may hold values from -6 to 6
- grad_out: bfloat16 [4096, 5120], P('row', 'col'), may hold values from -6 to 6
- pre_act: bfloat16 [4096, 13824], P('col', 'row'), may hold values from -6 to 6
- w_in: bfloat16 [13824, 5120], P('row', 'col'), may hold values from -0.078125 to 0.078125
- w_out: bfloat16 [13824, 5120], P('row', 'col'), may hold values from -0.0546875 to 0.0546875
- row_in_prev: float32 [13824], P('row'), may hold values from 204.8 to 24576, as said below
- col_in_prev: float32 [5120], P('col'), may hold values from 204.8 to 24576, as said below
- row_out_prev: float32 [13824], P('row'), may hold values from 204.8 to 24576, as said below
- col_out_prev: float32 [5120], P('col'), may hold values from 204.8 to 24576, as said below
Outputs:
- input_grad: bfloat16 [4096, 5120], P('row', 'col')
- update_in: float32 [13824, 5120], P('row', 'col')
- row_in: float32 [13824], P('row')
- col_in: float32 [5120], P('col')
- update_out: float32 [13824, 5120], P('row', 'col')
- row_out: float32 [13824], P('row')
- col_out: float32 [5120], P('col')
Inputs may be any that keep to these rules, and one draw needn't show every extreme that they name: `row_in_prev`: positive. `col_in_prev`: positive. `row_out_prev`: positive. `col_out_prev`: positive.
All inputs are finite; a program needn't handle non-finite values.
Results may differ from a plain program's by a relative error of at most 0.023.
Values may be sent and summed in bfloat16 or wider, within the bound.
A program may use at most 128 MiB of HBM per device.

v0:
```python
import math
import jax
import jax.numpy as jnp
from jax import lax
from jax.sharding import PartitionSpec as P

D = 5120
FF = 13824
decay_rate = 0.8
epsilon_sq = 1e-30
clip_limit = 0.25
gelu_coef = 0.044715
root_coef = math.sqrt(2.0 / math.pi)


def gelu_parts(pre_float):
    tanh_value = jnp.tanh(root_coef * (pre_float + gelu_coef * pre_float * pre_float * pre_float))
    value = 0.5 * pre_float * (1.0 + tanh_value)
    slope = 0.5 * (1.0 + tanh_value) + 0.5 * pre_float * (
        1.0 - tanh_value * tanh_value
    ) * root_coef * (1.0 + 3.0 * gelu_coef * pre_float * pre_float)
    return (value, slope)


def contract_last(left, right):
    return lax.dot_general(
        left, right, (((1,), (1,)), ((), ())), preferred_element_type=jnp.float32
    )


def contract_first(left, right):
    return lax.dot_general(
        left, right, (((0,), (0,)), ((), ())), preferred_element_type=jnp.float32
    )


def row_moment(row_sum, row_prev):
    return decay_rate * row_prev + (1.0 - decay_rate) * (row_sum / D + epsilon_sq)


def col_moment(col_sum, col_prev):
    return decay_rate * col_prev + (1.0 - decay_rate) * (col_sum / FF + epsilon_sq)


def per_device(
    inputs, grad_out, pre_act, w_in, w_out, row_in_prev, col_in_prev, row_out_prev, col_out_prev
):
    grad_all, input_all = (
        lax.all_gather(grad_out, "row", axis=0, tiled=True),
        lax.all_gather(inputs, "row", axis=0, tiled=True),
    )
    token_count = float(inputs.shape[0] * lax.axis_size("row"))
    rows_here = grad_all
    hidden_grad = lax.psum_scatter(
        contract_last(rows_here, w_out).astype(jnp.bfloat16), "col", scatter_dimension=0, tiled=True
    ).astype(jnp.float32)
    value, slope = gelu_parts(pre_act.astype(jnp.float32))
    act = value.astype(jnp.bfloat16)
    pre_grad = (hidden_grad * slope).astype(jnp.bfloat16)
    act_all, pre_grad_all = (
        lax.all_gather(act, "col", axis=0, tiled=True),
        lax.all_gather(pre_grad, "col", axis=0, tiled=True),
    )
    grad_w_out = contract_first(act_all, grad_all)
    grad_w_in = contract_first(pre_grad_all, input_all)
    rows_here = pre_grad_all
    input_sum = lax.psum_scatter(
        jnp.dot(rows_here, w_in, preferred_element_type=jnp.float32).astype(jnp.bfloat16),
        "row",
        scatter_dimension=0,
        tiled=True,
    )
    square_in = grad_w_in * grad_w_in
    square_out = grad_w_out * grad_w_out
    row_sums = lax.psum((jnp.sum(square_in, axis=1), jnp.sum(square_out, axis=1)), "col")
    row_in = row_moment(row_sums[0], row_in_prev)
    row_out = row_moment(row_sums[1], row_out_prev)
    col_sums = lax.psum((jnp.sum(square_in, axis=0), jnp.sum(square_out, axis=0)), "row")
    col_in = col_moment(col_sums[0], col_in_prev)
    col_out = col_moment(col_sums[1], col_out_prev)
    raw_in = grad_w_in / jnp.sqrt(row_in[:, None] * col_in[None, :] / token_count)
    raw_out = grad_w_out / jnp.sqrt(row_out[:, None] * col_out[None, :] / token_count)
    norms = lax.psum((jnp.sum(raw_in * raw_in), jnp.sum(raw_out * raw_out)), ("row", "col"))
    total_in = norms[0]
    total_out = norms[1]
    rms_in = jnp.sqrt(total_in / (FF * D))
    rms_out = jnp.sqrt(total_out / (FF * D))
    update_in = raw_in / jnp.maximum(1.0, rms_in / clip_limit)
    update_out = raw_out / jnp.maximum(1.0, rms_out / clip_limit)
    return (input_sum, update_in, row_in, col_in, update_out, row_out, col_out)


def solution(mesh):
    return jax.shard_map(
        per_device,
        mesh=mesh,
        in_specs=(
            P("row", "col"),
            P("row", "col"),
            P("col", "row"),
            P("row", "col"),
            P("row", "col"),
            P("row"),
            P("col"),
            P("row"),
            P("col"),
        ),
        out_specs=(
            P("row", "col"),
            P("row", "col"),
            P("row"),
            P("col"),
            P("row", "col"),
            P("row"),
            P("col"),
        ),
        check_vma=False,
    )
```

profile of v0, /device:TPU:1, one launch (start us, length us, event | category | flops | bytes accessed | tf_op | source)
XLA Modules:
  0.0 452.0 jit_solution(9500882296809639069)
XLA Ops:
  7.2 0.0 copy-start
  7.2 0.0 all-gather.5.cloned.1.call-start
  7.2 0.7 all-gather.5.cloned.1.call-update
  7.9 0.0 reduce-scatter.3.cloned.1.call-start
  8.0 59.3 %all-gather.5.cloned.1.call-done = bf16[4096,640]{1,0:T(8,128)(2,1)} async-done(((bf16[128,640]{1,0:T(8,128)(2,1)}), bf16[4096,640]{1,0:T(8,128)(2,1)}) %all-gather.5.cloned.1.call-update) | async-done | bytes 5242896 | tf_op jit(solution)/shard_map/all_gather | solution.py:49
  67.3 7.4 %convolution_convert_fusion.1 = bf16[4096,432]{0,1:T(8,128)(2,1)} fusion(bf16[4096,640]{1,0:T(8,128)(2,1)} %all-gather.5.cloned.1.call-done, bf16[432,640]{1,0:T(8,128)(2,1)} %param.13), kind=kOutput, calls=%fused_computation.1 | convolution fusion | flops 2266693632 | bytes 9334784 | tf_op jit(solution)/shard_map/dot_general | solution.py:26
  74.7 0.0 reduce-scatter.3.cloned.1.call-update
  74.7 0.0 all-gather.7.cloned.1.call-start
  74.7 48.2 %reduce-scatter.3.cloned.1.call-done = bf16[512,432]{0,1:T(8,128)(2,1)} async-done(((bf16[4096,432]{0,1:T(8,128)(2,1)}), bf16[512,432]{0,1:T(8,128)(2,1)}) %reduce-scatter.3.cloned.1.call-update) | async-done | bytes 442384 | tf_op jit(solution)/shard_map/reduce_scatter | solution.py:54
  123.0 2.6 fusion.7
  125.6 0.0 all-gather.7.cloned.1.call-update
  125.6 0.0 all-gather.11.cloned.1.call-start
  125.6 0.5 all-gather.11.cloned.1.call-update
  126.2 0.0 all-gather.9.cloned.1.call-start
  126.2 0.5 all-gather.9.cloned.1.call-update
  126.8 0.0 reduce-scatter.5.cloned.1.call-start
  126.8 46.8 %all-gather.7.cloned.1.call-done = bf16[4096,432]{0,1:T(8,128)(2,1)} async-done(((bf16[512,432]{0,1:T(8,128)(2,1)}), bf16[4096,432]{0,1:T(8,128)(2,1)}) %all-gather.7.cloned.1.call-update) | async-done | bytes 3538960 | tf_op jit(solution)/shard_map/all_gather | solution.py:62
  173.6 7.9 %convolution_convert_fusion = bf16[4096,640]{1,0:T(8,128)(2,1)} fusion(bf16[4096,432]{0,1:T(8,128)(2,1)} %all-gather.7.cloned.1.call-done, bf16[432,640]{1,0:T(8,128)(2,1)S(1)} %copy-done), kind=kOutput, calls=%fused_computation | convolution fusion | flops 2267545600 | bytes 9334784 | tf_op jit(solution)/shard_map/dot_general | solution.py:68
  181.5 0.0 reduce-scatter.5.cloned.1.call-update
  181.5 41.8 %all-gather.11.cloned.1.call-done = bf16[4096,432]{0,1:T(8,128)(2,1)} async-done(((bf16[512,432]{0,1:T(8,128)(2,1)}), bf16[4096,432]{0,1:T(8,128)(2,1)}) %all-gather.11.cloned.1.call-update) | async-done | bytes 3538960 | tf_op jit(solution)/shard_map/all_gather | solution.py:61
  223.3 6.6 %multiply_reduce_fusion.3 = (f32[432]{0:T(512)S(1)}, f32[640]{0:T(1024)S(1)}, f32[432,640]{1,0:T(8,128)S(1)}) fusion(bf16[4096,432]{0,1:T(8,128)(2,1)} %all-gather.11.cloned.1.call-done, bf16[4096,640]{1,0:T(8,128)(2,1)} %all-gather.5.cloned.1.call-done), kind=kOutput, calls=%fused_computation.16 | convolution fusion | flops 2265752576 | bytes 9892032 | tf_op jit(solution)/shard_map/dot_general | solution.py:32
  229.9 47.6 %all-gather.9.cloned.1.call-done = bf16[4096,640]{1,0:T(8,128)(2,1)} async-done(((bf16[128,640]{1,0:T(8,128)(2,1)}), bf16[4096,640]{1,0:T(8,128)(2,1)}) %all-gather.9.cloned.1.call-update) | async-done | bytes 5242896 | tf_op jit(solution)/shard_map/all_gather | solution.py:50
  277.6 6.6 %multiply_reduce_fusion.5 = (f32[432]{0:T(512)S(1)}, f32[640]{0:T(1024)S(1)}, f32[432,640]{1,0:T(8,128)S(1)}) fusion(bf16[4096,432]{0,1:T(8,128)(2,1)} %all-gather.7.cloned.1.call-done, bf16[4096,640]{1,0:T(8,128)(2,1)} %all-gather.9.cloned.1.call-done), kind=kOutput, calls=%fused_computation.18 | convolution fusion | flops 2265752576 | bytes 9892032 | tf_op jit(solution)/shard_map/dot_general | solution.py:32
  284.1 63.8 %all-reduce.1 = (f32[640]{0:T(1024)S(1)}, f32[640]{0:T(1024)S(1)}) all-reduce(f32[640]{0:T(1024)S(1)} %get-tuple-element.10, f32[640]{0:T(1024)S(1)} %get-tuple-element.8), channel_id=1, replica_groups=mesh['row'=32,'col'=8] {'row'}, use_global_device_ids=true, to_apply=%region_5.0 | all-reduce | flops 1280 | bytes 10240 | tf_op jit(solution)/shard_map/psum | solution.py:78
  347.9 13.8 %all-reduce.2 = (f32[432]{0:T(512)S(1)}, f32[432]{0:T(512)S(1)}) all-reduce(f32[432]{0:T(512)S(1)} %get-tuple-element.9, f32[432]{0:T(512)S(1)} %get-tuple-element.7), channel_id=1, replica_groups=mesh['row'=32,'col'=8] {'col'}, use_global_device_ids=true, to_apply=%region_3.0 | all-reduce | flops 864 | bytes 6912 | tf_op jit(solution)/shard_map/psum | solution.py:75
  361.8 0.0 copy-start.5
  361.8 0.0 copy-start.2
  361.8 1.1 multiply_reduce_fusion
  362.9 1.1 multiply_reduce_fusion.1
  364.0 77.3 %all-reduce = (f32[]{:T(128)}, f32[]{:T(128)}) all-reduce(f32[]{:T(128)} %multiply_reduce_fusion.1, f32[]{:T(128)} %multiply_reduce_fusion), channel_id=1, replica_groups=mesh['row'=32,'col'=8] {'row','col'}, use_global_device_ids=true, to_apply=%region_7.0 | all-reduce | flops 2 | bytes 16 | tf_op jit(solution)/shard_map/psum | solution.py:83
  442.7 1.2 fusion.12
  444.0 1.2 fusion.11
  (20 shorter events, 0.1 us)
Async XLA Ops:
  7.2 166.5 %copy-start = (bf16[432,640]{1,0:T(8,128)(2,1)S(1)}, bf16[432,640]{1,0:T(8,128)(2,1)}, u32[]{:S(2)}) copy-start(bf16[432,640]{1,0:T(8,128)(2,1)} %param.12) | copy-start | bytes 1658884
  7.2 60.1 %all-gather.5.cloned.1.call-start = ((), (), s32[]{:S(2)}) async-start(), calls=%async_computation.2 | async-start | bytes 5406720 | tf_op jit(solution)/shard_map/all_gather | solution.py:49
  7.9 115.1 %reduce-scatter.3.cloned.1.call-start = ((), (), s32[]{:S(2)}) async-start(), calls=%async_computation.3 | async-start | bytes 3981312 | tf_op jit(solution)/shard_map/reduce_scatter | solution.py:54
  74.7 48.3 %copy-start.1 = (bf16[512,432]{0,1:T(8,128)(2,1)S(1)}, bf16[512,432]{0,1:T(8,128)(2,1)}, u32[]{:S(2)}) copy-start(bf16[512,432]{0,1:T(8,128)(2,1)} %param.11) | copy-start | bytes 1327108
  74.7 98.9 %all-gather.7.cloned.1.call-start = ((), (), s32[]{:S(2)}) async-start(), calls=%async_computation.4 | async-start | bytes 3981312 | tf_op jit(solution)/shard_map/all_gather | solution.py:62
  125.6 97.7 %all-gather.11.cloned.1.call-start = ((), (), s32[]{:S(2)}) async-start(), calls=%async_computation.7 | async-start | bytes 3981312 | tf_op jit(solution)/shard_map/all_gather | solution.py:61
  126.2 151.4 %all-gather.9.cloned.1.call-start = ((), (), s32[]{:S(2)}) async-start(), calls=%async_computation.6 | async-start | bytes 5406720 | tf_op jit(solution)/shard_map/all_gather | solution.py:50
  126.8 318.4 %reduce-scatter.5.cloned.1.call-start = ((), (), s32[]{:S(2)}) async-start(), calls=%async_computation.5 | async-start | bytes 5406720 | tf_op jit(solution)/shard_map/reduce_scatter | solution.py:67
  229.9 131.9 %copy-start.8 = (f32[432]{0:T(512)S(1)}, f32[432]{0:T(512)}, u32[]{:S(2)}) copy-start(f32[432]{0:T(512)} %param.16) | copy-start | bytes 5188
  229.9 131.9 %copy-start.9 = (f32[432]{0:T(512)S(1)}, f32[432]{0:T(512)}, u32[]{:S(2)}) copy-start(f32[432]{0:T(512)} %param.14) | copy-start | bytes 5188
  229.9 131.9 %copy-start.6 = (f32[640]{0:T(1024)S(1)}, f32[640]{0:T(1024)}, u32[]{:S(2)}) copy-start(f32[640]{0:T(1024)} %param.17) | copy-start | bytes 7684
  229.9 131.9 %copy-start.7 = (f32[640]{0:T(1024)S(1)}, f32[640]{0:T(1024)}, u32[]{:S(2)}) copy-start(f32[640]{0:T(1024)} %param.15) | copy-start | bytes 7684
  361.8 80.9 %copy-start.4 = (f32[432]{0:T(512)}, f32[432]{0:T(512)S(1)}, u32[]{:S(2)}) copy-start(f32[432]{0:T(512)S(1)} %get-tuple-element.23) | copy-start | bytes 5188
  361.8 82.2 %copy-start.5 = (f32[432]{0:T(512)}, f32[432]{0:T(512)S(1)}, u32[]{:S(2)}) copy-start(f32[432]{0:T(512)S(1)} %get-tuple-element.24) | copy-start | bytes 5188
  361.8 80.9 %copy-start.2 = (f32[640]{0:T(1024)}, f32[640]{0:T(1024)S(1)}, u32[]{:S(2)}) copy-start(f32[640]{0:T(1024)S(1)} %get-tuple-element.21) | copy-start | bytes 7684
  361.8 82.1 %copy-start.3 = (f32[640]{0:T(1024)}, f32[640]{0:T(1024)S(1)}, u32[]{:S(2)}) copy-start(f32[640]{0:T(1024)S(1)} %get-tuple-element.22) | copy-start | bytes 7684
Sparse Core Ops, SparseCore 0:
  10.6 56.6 all-gather.4
  74.8 48.1 reduce-scatter.2
  125.7 47.8 all-gather.6
  176.0 47.2 all-gather.10
  226.0 51.4 all-gather.8
  282.5 89.6 reduce-scatter.4
where the time goes:
time: 452 us
  waiting for transfers between devices  246 us (54%)
  blocking collectives  155 us (34%)
  matrix products  28.4 us (6%)
  between operations  15.6 us (3%)
  other arithmetic  7.26 us (2%)
    psum x1, blocking collectives, per_device(): lax.psum((jnp.sum(raw_in * raw_in), jnp.sum(raw_out * raw_out)), ('row',...  77.3 us
    psum x1, blocking collectives, per_device(): lax.psum((jnp.sum(square_in, axis=0), jnp.sum(square_out, axis=0)), 'row')  63.8 us
    all_gather x1, waiting for transfers between devices, per_device(): lax.all_gather(grad_out, 'row', axis=0, tiled=True)  59.3 us
    reduce_scatter x1, waiting for transfers between devices, per_device(): lax.psum_scatter(contract_last(rows_here, w_out).astype(jnp.bfloat16), 'c...  48.2 us
    all_gather x1, waiting for transfers between devices, per_device(): lax.all_gather(inputs, 'row', axis=0, tiled=True)  47.6 us
    all_gather x1, waiting for transfers between devices, per_device(): lax.all_gather(pre_grad, 'col', axis=0, tiled=True)  46.8 us
    all_gather x1, waiting for transfers between devices, per_device(): lax.all_gather(act, 'col', axis=0, tiled=True)  41.8 us
    psum x1, blocking collectives, per_device(): lax.psum((jnp.sum(square_in, axis=1), jnp.sum(square_out, axis=1)), 'col')  13.8 us
  transfers between devices with their start and end apart: 6, of which 5 were waited for; matrix products, arithmetic and copies ran while one was open for 6% of the time, Pallas kernels for 0%

commit v1 on v0

--- a/solution.py
+++ b/solution.py
@@ -58,7 +58,9 @@
     act = value.astype(jnp.bfloat16)
     pre_grad = (hidden_grad * slope).astype(jnp.bfloat16)
     act_all, pre_grad_all = (
-        lax.all_gather(act, "col", axis=0, tiled=True),
+        jnp.concatenate(
+            lax.all_to_all(jnp.stack([act] * lax.axis_size("col")), "col", 0, 0), axis=0
+        ),
         lax.all_gather(pre_grad, "col", axis=0, tiled=True),
     )
     grad_w_out = contract_first(act_all, grad_all)

time: 452 us -> 475 us (1.051)
  waiting for transfers between devices: 246 us -> 261 us
    all_gather x1, waiting for transfers between devices: 46.8 us -> 111 us  [per_device(): lax.all_gather(pre_grad, 'col', axis=0, tiled=True)]
    all_gather x1 -> x0, waiting for transfers between devices: 41.8 us -> none  [per_device(): lax.all_gather(act, 'col', axis=0, tiled=True)]
    all_gather x1, waiting for transfers between devices: 47.6 us -> 40.4 us  [per_device(): lax.all_gather(inputs, 'row', axis=0, tiled=True)]
  transfers between devices with their start and end apart: 6 -> 6, of which waited for: 5 -> 4; matrix products, arithmetic and copies ran while one was open for 6% -> 6% of each run, Pallas kernels for 0% -> 0%
where the time goes in v1:
time: 475 us
  waiting for transfers between devices  261 us (55%)
  blocking collectives  155 us (33%)
  matrix products  27.3 us (6%)
  between operations  15.3 us (3%)
  other arithmetic  7.12 us (1%)
  starting transfers between devices  4.87 us (1%)
    all_gather x1, waiting for transfers between devices, per_device(): lax.all_gather(pre_grad, 'col', axis=0, tiled=True)  111 us
    psum x1, blocking collectives, per_device(): lax.psum((jnp.sum(raw_in * raw_in), jnp.sum(raw_out * raw_out)), ('row',...  77.3 us
    psum x1, blocking collectives, per_device(): lax.psum((jnp.sum(square_in, axis=0), jnp.sum(square_out, axis=0)), 'row')  63.8 us
    all_gather x1, waiting for transfers between devices, per_device(): lax.all_gather(grad_out, 'row', axis=0, tiled=True)  59.3 us
    reduce_scatter x1, waiting for transfers between devices, per_device(): lax.psum_scatter(contract_last(rows_here, w_out).astype(jnp.bfloat16), 'c...  48.2 us
    all_gather x1, waiting for transfers between devices, per_device(): lax.all_gather(inputs, 'row', axis=0, tiled=True)  40.4 us
    psum x1, blocking collectives, per_device(): lax.psum((jnp.sum(square_in, axis=1), jnp.sum(square_out, axis=1)), 'col')  13.8 us
    dot_general x2, matrix products, contract_first(): lax.dot_general(left, right, (((0,), (0,)), ((), ())), preferred_element_...  12.1 us
  transfers between devices with their start and end apart: 6, of which 4 were waited for; matrix products, arithmetic and copies ran while one was open for 6% of the time, Pallas kernels for 0%

profile of v1, /device:TPU:1, one launch (start us, length us, event | category | flops | bytes accessed | tf_op | source)
XLA Modules:
  0.0 474.7 jit_solution(12795899404350975092)
XLA Ops:
  7.2 0.0 copy-start
  7.2 0.0 all-gather.4.cloned.1.call-start
  7.2 0.7 all-gather.4.cloned.1.call-update
  7.9 0.0 reduce-scatter.3.cloned.1.call-start
  8.0 59.3 %all-gather.4.cloned.1.call-done = bf16[4096,640]{1,0:T(8,128)(2,1)} async-done(((bf16[128,640]{1,0:T(8,128)(2,1)}), bf16[4096,640]{1,0:T(8,128)(2,1)}) %all-gather.4.cloned.1.call-update) | async-done | bytes 5242896 | tf_op jit(solution)/shard_map/all_gather | solution.py:49
  67.3 7.4 %convolution_convert_fusion.1 = bf16[4096,432]{0,1:T(8,128)(2,1)} fusion(bf16[4096,640]{1,0:T(8,128)(2,1)} %all-gather.4.cloned.1.call-done, bf16[432,640]{1,0:T(8,128)(2,1)} %param.13), kind=kOutput, calls=%fused_computation.1 | convolution fusion | flops 2266693632 | bytes 9334784 | tf_op jit(solution)/shard_map/dot_general | solution.py:26
  74.7 0.0 reduce-scatter.3.cloned.1.call-update
  74.7 0.0 all-gather.6.cloned.1.call-start
  74.7 48.2 %reduce-scatter.3.cloned.1.call-done = bf16[512,432]{0,1:T(8,128)(2,1)} async-done(((bf16[4096,432]{0,1:T(8,128)(2,1)}), bf16[512,432]{0,1:T(8,128)(2,1)}) %reduce-scatter.3.cloned.1.call-update) | async-done | bytes 442384 | tf_op jit(solution)/shard_map/reduce_scatter | solution.py:54
  123.0 2.5 fusion.7
  125.4 0.0 all-gather.6.cloned.1.call-update
  125.5 0.0 all-gather.8.cloned.1.call-start
  125.5 0.5 all-gather.8.cloned.1.call-update
  126.0 2.1 stack.2
  128.2 4.5 all-to-all-start
  132.7 0.2 reduce-scatter.5.cloned.1.call-start
  132.9 111.3 %all-gather.6.cloned.1.call-done = bf16[4096,432]{0,1:T(8,128)(2,1)} async-done(((bf16[512,432]{0,1:T(8,128)(2,1)}), bf16[4096,432]{0,1:T(8,128)(2,1)}) %all-gather.6.cloned.1.call-update) | async-done | bytes 3538960 | tf_op jit(solution)/shard_map/all_gather | solution.py:64
  244.2 7.9 %convolution_convert_fusion = bf16[4096,640]{1,0:T(8,128)(2,1)} fusion(bf16[4096,432]{0,1:T(8,128)(2,1)} %all-gather.6.cloned.1.call-done, bf16[432,640]{1,0:T(8,128)(2,1)S(1)} %copy-done), kind=kOutput, calls=%fused_computation | convolution fusion | flops 2267545600 | bytes 9334784 | tf_op jit(solution)/shard_map/dot_general | solution.py:70
  252.1 0.0 reduce-scatter.5.cloned.1.call-update
  252.1 2.4 copy.18
  254.5 5.5 %multiply_reduce_fusion.3 = (f32[432]{0:T(512)S(1)}, f32[640]{0:T(1024)S(1)}, f32[432,640]{1,0:T(8,128)S(1)}) fusion(bf16[4096,432]{0,1:T(8,128)(2,1)S(1)} %bitcast.10, bf16[4096,640]{1,0:T(8,128)(2,1)} %all-gather.4.cloned.1.call-done), kind=kOutput, calls=%fused_computation.16 | convolution fusion | flops 2265752576 | bytes 9892032 | tf_op jit(solution)/shard_map/dot_general | solution.py:32
  260.1 40.4 %all-gather.8.cloned.1.call-done = bf16[4096,640]{1,0:T(8,128)(2,1)} async-done(((bf16[128,640]{1,0:T(8,128)(2,1)}), bf16[4096,640]{1,0:T(8,128)(2,1)}) %all-gather.8.cloned.1.call-update) | async-done | bytes 5242896 | tf_op jit(solution)/shard_map/all_gather | solution.py:50
  300.5 6.6 %multiply_reduce_fusion.5 = (f32[432]{0:T(512)S(1)}, f32[640]{0:T(1024)S(1)}, f32[432,640]{1,0:T(8,128)S(1)}) fusion(bf16[4096,432]{0,1:T(8,128)(2,1)} %all-gather.6.cloned.1.call-done, bf16[4096,640]{1,0:T(8,128)(2,1)} %all-gather.8.cloned.1.call-done), kind=kOutput, calls=%fused_computation.18 | convolution fusion | flops 2265752576 | bytes 9892032 | tf_op jit(solution)/shard_map/dot_general | solution.py:32
  307.1 63.8 %all-reduce.1 = (f32[640]{0:T(1024)S(1)}, f32[640]{0:T(1024)S(1)}) all-reduce(f32[640]{0:T(1024)S(1)} %get-tuple-element.10, f32[640]{0:T(1024)S(1)} %get-tuple-element.8), channel_id=1, replica_groups=mesh['row'=32,'col'=8] {'row'}, use_global_device_ids=true, to_apply=%region_5.0 | all-reduce | flops 1280 | bytes 10240 | tf_op jit(solution)/shard_map/psum | solution.py:80
  370.9 13.8 %all-reduce.2 = (f32[432]{0:T(512)S(1)}, f32[432]{0:T(512)S(1)}) all-reduce(f32[432]{0:T(512)S(1)} %get-tuple-element.9, f32[432]{0:T(512)S(1)} %get-tuple-element.7), channel_id=1, replica_groups=mesh['row'=32,'col'=8] {'col'}, use_global_device_ids=true, to_apply=%region_3.0 | all-reduce | flops 864 | bytes 6912 | tf_op jit(solution)/shard_map/psum | solution.py:77
  384.8 0.0 copy-start.5
  384.8 0.0 copy-start.2
  384.8 1.1 multiply_reduce_fusion
  385.9 1.1 multiply_reduce_fusion.1
  387.0 77.3 %all-reduce = (f32[]{:T(128)}, f32[]{:T(128)}) all-reduce(f32[]{:T(128)} %multiply_reduce_fusion.1, f32[]{:T(128)} %multiply_reduce_fusion), channel_id=1, replica_groups=mesh['row'=32,'col'=8] {'row','col'}, use_global_device_ids=true, to_apply=%region_7.0 | all-reduce | flops 2 | bytes 16 | tf_op jit(solution)/shard_map/psum | solution.py:85
  465.7 1.2 fusion.12
  467.0 1.2 fusion.11
  (21 shorter events, 0.1 us)
Async XLA Ops:
  7.2 237.0 %copy-start = (bf16[432,640]{1,0:T(8,128)(2,1)S(1)}, bf16[432,640]{1,0:T(8,128)(2,1)}, u32[]{:S(2)}) copy-start(bf16[432,640]{1,0:T(8,128)(2,1)} %param.12) | copy-start | bytes 1658884
  7.2 60.1 %all-gather.4.cloned.1.call-start = ((), (), s32[]{:S(2)}) async-start(), calls=%async_computation.3 | async-start | bytes 5406720 | tf_op jit(solution)/shard_map/all_gather | solution.py:49
  7.9 115.1 %reduce-scatter.3.cloned.1.call-start = ((), (), s32[]{:S(2)}) async-start(), calls=%async_computation.4 | async-start | bytes 3981312 | tf_op jit(solution)/shard_map/reduce_scatter | solution.py:54
  74.7 48.3 %copy-start.1 = (bf16[512,432]{0,1:T(8,128)(2,1)S(1)}, bf16[512,432]{0,1:T(8,128)(2,1)}, u32[]{:S(2)}) copy-start(bf16[512,432]{0,1:T(8,128)(2,1)} %param.11) | copy-start | bytes 1327108
  74.7 169.5 %all-gather.6.cloned.1.call-start = ((), (), s32[]{:S(2)}) async-start(), calls=%async_computation.5 | async-start | bytes 3981312 | tf_op jit(solution)/shard_map/all_gather | solution.py:64
  125.5 175.1 %all-gather.8.cloned.1.call-start = ((), (), s32[]{:S(2)}) async-start(), calls=%async_computation.7 | async-start | bytes 5406720 | tf_op jit(solution)/shard_map/all_gather | solution.py:50
  128.2 123.9 %all-to-all-start = ((bf16[8,512,432]{1,2,0:T(8,128)(2,1)}), bf16[8,512,432]{1,2,0:T(8,128)(2,1)}, u32[]{:S(2)}, u32[]{:S(2)}) async-start(bf16[8,512,432]{1,2,0:T(8,128)(2,1)} %stack.2), calls=%async_computation.2 | async-start | bytes 7077888 | tf_op jit(solution)/shard_map/all_to_all | solution.py:62
  132.7 335.5 %reduce-scatter.5.cloned.1.call-start = ((), (), s32[]{:S(2)}) async-start(), calls=%async_computation.6 | async-start | bytes 5406720 | tf_op jit(solution)/shard_map/reduce_scatter | solution.py:69
  260.1 124.7 %copy-start.8 = (f32[432]{0:T(512)S(1)}, f32[432]{0:T(512)}, u32[]{:S(2)}) copy-start(f32[432]{0:T(512)} %param.16) | copy-start | bytes 5188
  260.1 124.7 %copy-start.9 = (f32[432]{0:T(512)S(1)}, f32[432]{0:T(512)}, u32[]{:S(2)}) copy-start(f32[432]{0:T(512)} %param.14) | copy-start | bytes 5188
  260.1 124.7 %copy-start.6 = (f32[640]{0:T(1024)S(1)}, f32[640]{0:T(1024)}, u32[]{:S(2)}) copy-start(f32[640]{0:T(1024)} %param.17) | copy-start | bytes 7684
  260.1 124.7 %copy-start.7 = (f32[640]{0:T(1024)S(1)}, f32[640]{0:T(1024)}, u32[]{:S(2)}) copy-start(f32[640]{0:T(1024)} %param.15) | copy-start | bytes 7684
  384.8 81.0 %copy-start.4 = (f32[432]{0:T(512)}, f32[432]{0:T(512)S(1)}, u32[]{:S(2)}) copy-start(f32[432]{0:T(512)S(1)} %get-tuple-element.23) | copy-start | bytes 5188
  384.8 82.2 %copy-start.5 = (f32[432]{0:T(512)}, f32[432]{0:T(512)S(1)}, u32[]{:S(2)}) copy-start(f32[432]{0:T(512)S(1)} %get-tuple-element.24) | copy-start | bytes 5188
  384.8 80.9 %copy-start.2 = (f32[640]{0:T(1024)}, f32[640]{0:T(1024)S(1)}, u32[]{:S(2)}) copy-start(f32[640]{0:T(1024)S(1)} %get-tuple-element.21) | copy-start | bytes 7684
  384.8 82.1 %copy-start.3 = (f32[640]{0:T(1024)}, f32[640]{0:T(1024)S(1)}, u32[]{:S(2)}) copy-start(f32[640]{0:T(1024)S(1)} %get-tuple-element.22) | copy-start | bytes 7684
Sparse Core Ops, SparseCore 0:
  10.6 56.6 all-gather.3
  74.8 48.1 reduce-scatter.2
  125.6 118.5 all-gather.5
  246.9 53.5 all-gather.7
  305.5 89.6 reduce-scatter.4
